TPU v7x, 32 devices: a whole 2x2x4 slice. The times are simulated.
32 devices in a mesh: mode: 8 (over z, x), row: 4 (over y, core).
Axes of the slice: x: 2, y: 2, z: 4, core: 2. Of those that a mesh axis runs over, the one named last changes fastest.
Arguments:
- forward: bfloat16 [64, 8, 2, 512], P('mode', 'row'), may hold values from -6 to 6
- backward: bfloat16 [64, 8, 2, 512], P('mode', 'row'), may hold values from -6 to 6
- propagator: bfloat16 [2, 512, 512], replicated, may hold values from -0.1875 to 0.1875
- row_taps: float32 [2, 3], replicated, may hold values from -3 to 3
- phase_masks: float32 [7, 8, 512], P(None, 'row'), may hold values from -3.140625 to 3.140625
- plane_index: int32 [4], replicated, may hold values from 0 to 6
- wave_ratio: float32 [4], replicated, may hold values from 0.7 to 1.4
- pair_list: int32 [80, 2], replicated, may hold values from 0 to 15, as said below
Outputs:
- coupling: float32 [2, 64, 64], P(None, 'mode')
- mask_grad: float32 [4, 8, 512], P(None, 'row')
Inputs may be any that keep to these rules, and one draw needn't show every extreme that they name: `pair_list`: each row names a target group and a forward group; no pair appears twice and every group is paired with itself; 80 pairs in all.
All inputs are finite; a program needn't handle non-finite values.
Results may differ from a plain program's by a relative error of at most 0.0078.
Values may be sent and summed in bfloat16 or wider, within the bound.
No kernel may reach another device: no remote copies, remote signals or barrier semaphores. Data moves between devices by JAX's collectives and lax.ppermute only.
A program may use at most 64 MiB of HBM per device.

v0:
```python
import math
import jax
import jax.numpy as jnp
from jax import lax
from jax.sharding import PartitionSpec as P

NG = 16


def padded_2(array, sides, width):
    for axis, dim in sides:
        peers, length = (lax.axis_size(axis), array.shape[dim])
        up = [(i, (i + 1) % peers) for i in range(peers - 1)]
        down = [(j, i) for i, j in up]
        last = lax.slice_in_dim(array, length - width, length, axis=dim)
        leading = lax.slice_in_dim(array, 0, width, axis=dim)
        before = lax.ppermute(last, axis, up)
        after = lax.ppermute(leading, axis, down)
        array = jnp.concatenate([before, array, after], axis=dim)
    return array


def chosen_phases(phase_masks, plane_index, wave_ratio):
    planes = jnp.arange(phase_masks.shape[0], dtype=jnp.int32)
    selector = (plane_index[:, None] == planes[None, :]).astype(jnp.float32)
    picked = jnp.einsum("wp,prc->wrc", selector, phase_masks, precision=lax.Precision.HIGHEST)
    return picked * wave_ratio[:, None, None]


def apply_mask(forward, phases):
    mode_total, row_total, _, width = forward.shape
    wave_total = phases.shape[0]
    shaped = forward.astype(jnp.float32).reshape(
        mode_total // wave_total, wave_total, row_total, 2, width
    )
    cosine = jnp.cos(phases)[None]
    sine = jnp.sin(phases)[None]
    real_part = shaped[:, :, :, 0] * cosine - shaped[:, :, :, 1] * sine
    imag_part = shaped[:, :, :, 0] * sine + shaped[:, :, :, 1] * cosine
    return jnp.stack([real_part, imag_part], axis=3).reshape(forward.shape).astype(jnp.bfloat16)


def forward_matrix(propagator):
    top_half = jnp.concatenate([propagator[0], propagator[1]], axis=1)
    low_half = jnp.concatenate([-propagator[1], propagator[0]], axis=1)
    return jnp.concatenate([top_half, low_half], axis=0)


def backward_matrix(propagator):
    top_half = jnp.concatenate([propagator[0].T, -propagator[1].T], axis=1)
    low_half = jnp.concatenate([propagator[1].T, propagator[0].T], axis=1)
    return jnp.concatenate([top_half, low_half], axis=0)


def propagate(fields, matrix):
    width = fields.shape[-1]
    result = jnp.dot(fields.reshape(-1, 2 * width), matrix, preferred_element_type=jnp.float32)
    return result.reshape(fields.shape)


def row_stencil(padded, row_taps, adjoint):
    values = padded.astype(jnp.float32)
    below_rows = values[:, :-2]
    center = values[:, 1:-1]
    above_rows = values[:, 2:]
    tap_real = row_taps[0]
    tap_imag = row_taps[1]
    if adjoint:
        sources = (above_rows, center, below_rows)
        tap_imag = -tap_imag
    else:
        sources = (below_rows, center, above_rows)
    real_sum = jnp.zeros(center[:, :, 0].shape, jnp.float32)
    imag_sum = jnp.zeros(center[:, :, 0].shape, jnp.float32)
    for position in range(3):
        source = sources[position]
        real_sum = (
            real_sum + tap_real[position] * source[:, :, 0] - tap_imag[position] * source[:, :, 1]
        )
        imag_sum = (
            imag_sum + tap_real[position] * source[:, :, 1] + tap_imag[position] * source[:, :, 0]
        )
    return jnp.stack([real_sum, imag_sum], axis=2)


def times_i(fields):
    return jnp.stack([-fields[:, :, 1], fields[:, :, 0]], axis=2)


def times_minus_i(fields):
    return jnp.stack([fields[:, :, 1], -fields[:, :, 0]], axis=2)


def body(forward, backward, propagator, row_taps, phase_masks, plane_index, wave_ratio, pair_list):
    local_modes, local_rows, _, width = forward.shape
    wave_total = wave_ratio.shape[0]
    mode_total = local_modes * lax.axis_size("mode")
    row_total = local_rows * lax.axis_size("row")
    group_size = mode_total // NG
    phases = chosen_phases(phase_masks, plane_index, wave_ratio)
    masked = apply_mask(forward, phases)
    spread = propagate(masked, forward_matrix(propagator)).astype(jnp.bfloat16)
    padded = padded_2(spread, (("row", 1),), 1)
    field = row_stencil(padded, row_taps, False).astype(jnp.bfloat16)
    field_flat = field.reshape(local_modes, -1)
    field_turned = times_minus_i(field).reshape(local_modes, -1)
    group_ids = jnp.arange(NG, dtype=jnp.int32)
    hits = (pair_list[:, 0][:, None, None] == group_ids[None, :, None]) & (
        pair_list[:, 1][:, None, None] == group_ids[None, None, :]
    )
    pair_matrix = jnp.sum(hits.astype(jnp.float32), axis=0)
    own_modes = lax.axis_index("mode") * local_modes + jnp.arange(local_modes, dtype=jnp.int32)
    own_onehot = ((own_modes // group_size)[:, None] == group_ids[None, :]).astype(jnp.float32)
    target_groups = jnp.arange(mode_total, dtype=jnp.int32) // group_size
    target_onehot = (target_groups[:, None] == group_ids[None, :]).astype(jnp.float32)
    own_pairs = jnp.dot(own_onehot, pair_matrix.T, precision=lax.Precision.HIGHEST)
    column_mask = jnp.dot(own_pairs, target_onehot.T, precision=lax.Precision.HIGHEST)
    shard_rows = lax.all_gather(backward, "mode", axis=0, tiled=True)
    rows_flat = shard_rows.reshape(shard_rows.shape[0], -1)
    real_part = jnp.einsum("nd,kd->nk", field_flat, rows_flat, preferred_element_type=jnp.float32)
    imag_part = jnp.einsum("nd,kd->nk", field_turned, rows_flat, preferred_element_type=jnp.float32)
    block = jnp.stack([real_part, imag_part])
    match_sum = lax.psum(block, "row")
    coupling = match_sum * (1.0 / math.sqrt(row_total * width)) * column_mask[None, :, :]
    weights = coupling.astype(jnp.bfloat16)
    shard_rows = lax.all_gather(backward, "mode", axis=0, tiled=True)
    row_count = shard_rows.shape[0]
    rows_flat = shard_rows.reshape(row_count, -1)
    rows_turned = times_i(shard_rows).reshape(row_count, -1)
    weight_real = weights[0]
    weight_imag = weights[1]
    running = jnp.dot(weight_real, rows_flat, preferred_element_type=jnp.float32)
    gathered = running + jnp.dot(weight_imag, rows_turned, preferred_element_type=jnp.float32)
    gathered = (
        (gathered * (1.0 / math.sqrt(mode_total))).astype(jnp.bfloat16).reshape(forward.shape)
    )
    padded_back = padded_2(gathered, (("row", 1),), 1)
    pulled = row_stencil(padded_back, row_taps, True).astype(jnp.bfloat16)
    adjoint = propagate(pulled, backward_matrix(propagator))
    masked_float = masked.astype(jnp.float32)
    term = masked_float[:, :, 1] * adjoint[:, :, 0] - masked_float[:, :, 0] * adjoint[:, :, 1]
    partial_grad = jnp.sum(
        term.reshape(local_modes // wave_total, wave_total, local_rows, width), axis=0
    )
    summed = lax.psum(partial_grad, "mode")
    mask_grad = summed * (-2.0 / math.sqrt(mode_total))
    return (coupling, mask_grad)


def solution(mesh):
    in_specs = (
        P("mode", "row", None, None),
        P("mode", "row", None, None),
        P(),
        P(),
        P(None, "row", None),
        P(),
        P(),
        P(),
    )
    out_specs = (P(None, "mode", None), P(None, "row", None))
    return jax.shard_map(body, mesh=mesh, in_specs=in_specs, out_specs=out_specs, check_vma=False)
```

profile of v0, /device:TPU:0, one launch (start us, length us, event | category | flops | bytes accessed | tf_op | source)
XLA Modules:
  0.0 117.6 jit_solution(7645582533571077190)
XLA Ops:
  0.6 0.0 copy-start
  0.6 0.0 copy-start.1
  0.7 0.0 copy-start.2
  0.7 0.0 copy-start.7
  0.7 0.0 copy-start.6
  0.7 2.7 %slice_bitcast_fusion = (bf16[512,512]{0,1:T(8,128)(2,1)}, bf16[512,512]{0,1:T(8,128)(2,1)}, bf16[512,512]{1,0:T(8,128)(2,1)}, bf16[512,512]{1,0:T(8,128)(2,1)}) fusion(bf16[2,512,512]{2,1,0:T(8,128)(2,1)} %param.10), kind=kLoop, calls=%fused_computation.10 | loop fusion | bytes 3145728 | tf_op jit(solution)/shard_map/transpose | solution.py:50
  3.4 0.0 copy-done.1
  3.4 0.9 fusion.19
  4.3 0.0 copy-done.2
  4.3 0.0 copy-done
  4.4 0.0 copy-done.7
  4.4 0.0 copy-done.6
  4.4 0.3 fusion.26
  4.8 1.8 %maximum_bitcast_fusion = bf16[1024,1024]{0,1:T(8,128)(2,1)S(1)} fusion(bf16[512,512]{1,0:T(8,128)(2,1)} %get-tuple-element.13, bf16[512,512]{1,0:T(8,128)(2,1)} %fusion.19, bf16[512,512]{1,0:T(8,128)(2,1)} %get-tuple-element.12), kind=kLoop, calls=%fused_computation.3 | loop fusion | flops 8388608 | bytes 3670016 | tf_op jit(solution)/shard_map/dot_general | solution.py:57
  6.6 2.6 %copy.33 = bf16[1024,1024]{1,0:T(8,128)(2,1)} copy(bf16[1024,1024]{0,1:T(8,128)(2,1)S(1)} %maximum_bitcast_fusion) | data formatting | bytes 4194304 | tf_op jit(solution)/shard_map/dot_general | solution.py:57
  9.2 0.0 copy-start.3
  9.2 0.0 copy-start.5
  9.2 0.0 copy-start.4
  9.2 2.3 %convolution_convert_fusion = bf16[8,2,2,512]{3,0,2,1:T(8,128)(2,1)S(1)} fusion(bf16[8,2,1024,1]{2,0,3,1:T(8,128)(2,1)S(1)} %bitcast.95, bf16[2,512,1024,1]{2,1,0,3:T(8,128)(2,1)} %bitcast.92), kind=kOutput, calls=%fused_computation.5 | convolution fusion | flops 33570816 | bytes 2162688 | tf_op jit(solution)/shard_map/dot_general | solution.py:57
  11.5 2.4 %collective-permute-start = (bf16[8,1,2,512]{3,0,2,1:T(8,128)(2,1)S(1)}, bf16[8,1,2,512]{3,0,2,1:T(8,128)(2,1)S(1)}, u32[]{:S(2)}, u32[]{:S(2)}) collective-permute-start(bf16[8,1,2,512]{3,0,2,1:T(8,128)(2,1)S(1)} %get-tuple-element.22), channel_id=1, source_target_pairs={{0,1},{1,2},{2,3},{4,5},{5,6},{6,7},{8,9},{9,10},{10,11},{12,13},{... | collective-permute-start | bytes 49160 | tf_op jit(solution)/shard_map/ppermute | solution.py:17
  13.9 1.3 %collective-permute-start.1 = (bf16[8,1,2,512]{3,0,2,1:T(8,128)(2,1)S(1)}, bf16[8,1,2,512]{3,0,2,1:T(8,128)(2,1)S(1)}, u32[]{:S(2)}, u32[]{:S(2)}) collective-permute-start(bf16[8,1,2,512]{3,0,2,1:T(8,128)(2,1)S(1)} %get-tuple-element.23), channel_id=1, source_target_pairs={{1,0},{2,1},{3,2},{5,4},{6,5},{7,6},{9,8},{10,9},{11,10},{13,12},{... | collective-permute-start | bytes 49160 | tf_op jit(solution)/shard_map/ppermute | solution.py:18
  15.2 0.8 fusion.20
  16.0 0.0 copy-done.3
  16.0 31.9 %all_gather.4 = bf16[64,2,2,512]{3,0,2,1:T(8,128)(2,1)S(1)} all-gather(bf16[8,2,2,512]{3,0,2,1:T(8,128)(2,1)S(1)} %copy.34), channel_id=1, replica_groups=mesh['mode'=8,'row'=4] {'mode'}, dimensions={0}, use_global_device_ids=true | all-gather | bytes 294912 | tf_op jit(solution)/shard_map/all_gather | solution.py:118
  47.9 0.0 copy-done.5
  48.0 0.0 copy-done.4
  48.0 0.1 convert_reduce_fusion
  48.1 0.2 fusion.11
  48.3 0.2 convolution_multiply_fusion.1
  48.5 0.1 pad_maximum_fusion
  48.6 1.8 %maximum_maximum_fusion = bf16[1024,1024]{0,1:T(8,128)(2,1)S(1)} fusion(bf16[512,512]{0,1:T(8,128)(2,1)} %get-tuple-element.11, bf16[512,512]{0,1:T(8,128)(2,1)} %get-tuple-element.10, bf16[512,512]{0,1:T(8,128)(2,1)} %fusion.20), kind=kLoop, calls=%fused_computation.4 | loop fusion | flops 8388608 | bytes 3670016 | tf_op jit(solution)/shard_map/concatenate | solution.py:52
  50.4 0.7 fusion.27
  51.0 0.3 copy.35
  51.3 0.2 reshape.169
  51.5 0.3 copy.36
  51.8 0.2 reshape.170
  52.0 0.0 collective-permute-done
  52.0 0.0 collective-permute-done.1
  52.0 3.7 %fusion.22 = (bf16[8,2,1,512]{3,0,2,1:T(8,128)(2,1)S(1)}, bf16[8,2,1,512]{3,0,2,1:T(8,128)(2,1)S(1)}) fusion(f32[8,4,2,512]{3,0,2,1:T(8,128)S(1)} %maximum_convert_fusion, f32[]{:T(128)} %bitcast.16, f32[]{:T(128)} %bitcast.15, f32[]{:T(128)} %bitcast.14, f32[]{:T(128)} %bitcast.13, f32[]{:T(128)} %bitcast.12, f32[]{:T(128)} %bitcast), kind=kLoop, calls=%fused_computation.70 | loop fusion | flops 106496 | bytes 229400 | tf_op jit(solution)/shard_map/neg | solution.py:91
  55.7 3.7 %add_convert_fusion.1 = bf16[8,2,1,512]{3,0,2,1:T(8,128)(2,1)S(1)} fusion(f32[8,4,2,512]{3,0,2,1:T(8,128)S(1)} %maximum_convert_fusion, f32[]{:T(128)} %bitcast.16, f32[]{:T(128)} %bitcast.15, f32[]{:T(128)} %bitcast.14, f32[]{:T(128)} %bitcast.13, f32[]{:T(128)} %bitcast.12, f32[]{:T(128)} %bitcast), kind=kLoop, calls=%fused_computation.33 | loop fusion | flops 98304 | bytes 213016 | tf_op jit(solution)/shard_map/slice | solution.py:91
  59.5 0.2 convolution_bitcast_fusion.1
  59.7 0.2 convolution_bitcast_fusion
  59.8 7.7 %psum.14 = f32[2,8,64]{2,1,0:T(8,128)S(1)} all-reduce(f32[2,8,64]{2,1,0:T(8,128)S(1)} %pad_maximum_fusion.2), channel_id=1, replica_groups=mesh['mode'=8,'row'=4] {'row'}, use_global_device_ids=true, to_apply=%region_0.0 | all-reduce | flops 1024 | bytes 8192 | tf_op jit(solution)/shard_map/psum | solution.py:123
  67.6 0.6 fusion.21
  68.2 0.1 fusion.12
  68.3 0.2 fusion.1
  68.5 2.3 %collective-permute-start.2 = (bf16[8,1,2,512]{3,0,2,1:T(8,128)(2,1)S(1)}, bf16[8,1,2,512]{3,0,2,1:T(8,128)(2,1)S(1)}, u32[]{:S(2)}, u32[]{:S(2)}) collective-permute-start(bf16[8,1,2,512]{3,0,2,1:T(8,128)(2,1)S(1)} %get-tuple-element.20), channel_id=1, source_target_pairs={{0,1},{1,2},{2,3},{4,5},{5,6},{6,7},{8,9},{9,10},{10,11},{12,13},{... | collective-permute-start | bytes 49160 | tf_op jit(solution)/shard_map/ppermute | solution.py:17
  70.8 1.3 %collective-permute-start.3 = (bf16[8,1,2,512]{3,0,2,1:T(8,128)(2,1)S(1)}, bf16[8,1,2,512]{3,0,2,1:T(8,128)(2,1)S(1)}, u32[]{:S(2)}, u32[]{:S(2)}) collective-permute-start(bf16[8,1,2,512]{3,0,2,1:T(8,128)(2,1)S(1)} %get-tuple-element.21), channel_id=1, source_target_pairs={{1,0},{2,1},{3,2},{5,4},{6,5},{7,6},{9,8},{10,9},{11,10},{13,12},{... | collective-permute-start | bytes 49160 | tf_op jit(solution)/shard_map/ppermute | solution.py:18
  72.1 0.7 fusion.28
  72.8 0.0 collective-permute-done.2
  72.8 2.6 %collective-permute-done.3 = bf16[8,1,2,512]{3,0,2,1:T(8,128)(2,1)S(1)} collective-permute-done((bf16[8,1,2,512]{3,0,2,1:T(8,128)(2,1)S(1)}, bf16[8,1,2,512]{3,0,2,1:T(8,128)(2,1)S(1)}, u32[]{:S(2)}, u32[]{:S(2)}) %collective-permute-start.3) | collective-permute-done | bytes 16416 | tf_op jit(solution)/shard_map/ppermute | solution.py:18
  75.4 3.8 %subtract_convert_fusion = (bf16[8,2,1,512]{3,0,2,1:T(8,128)(2,1)S(1)}, bf16[8,2,1,512]{3,0,2,1:T(8,128)(2,1)S(1)}) fusion(f32[8,4,2,512]{3,0,2,1:T(8,128)S(1)} %maximum_convert_fusion.1, f32[]{:T(128)} %bitcast.30, f32[]{:T(128)} %bitcast.29, f32[]{:T(128)} %bitcast.28, f32[]{:T(128)} %bitcast.15, f32[]{:T(128)} %bitcast.13, f32[]{:T(128)} %bitcast), kind=kLoop, calls=%fused_computation.31 | loop fusion | flops 196608 | bytes 229400 | tf_op jit(solution)/shard_map/convert.1
  79.2 0.6 fusion.29
  79.9 37.1 %psum.15 = f32[4,2,512]{2,0,1:T(4,128)S(1)} all-reduce(f32[4,2,512]{2,0,1:T(4,128)S(1)} %reduce_sum.19), channel_id=1, replica_groups=mesh['mode'=8,'row'=4] {'mode'}, use_global_device_ids=true, to_apply=%region_3.4 | all-reduce | flops 4096 | bytes 32768 | tf_op jit(solution)/shard_map/psum | solution.py:145
  117.0 0.6 copy.37
  (24 shorter events, 0.3 us)
Async XLA Ops:
  0.6 3.7 %copy-start = (f32[7,2,512]{2,1,0:T(2,128)S(1)}, f32[7,2,512]{2,1,0:T(2,128)}, u32[]{:S(2)}) copy-start(f32[7,2,512]{2,1,0:T(2,128)} %param.12) | copy-start | bytes 86020
  0.6 2.8 %copy-start.1 = (bf16[2,512,512]{2,1,0:T(8,128)(2,1)S(1)}, bf16[2,512,512]{2,1,0:T(8,128)(2,1)}, u32[]{:S(2)}) copy-start(bf16[2,512,512]{2,1,0:T(8,128)(2,1)} %param.10) | copy-start | bytes 3145732
  0.7 3.6 %copy-start.2 = (bf16[8,2,2,512]{3,2,1,0:T(2,128)(2,1)S(1)}, bf16[8,2,2,512]{3,2,1,0:T(2,128)(2,1)}, u32[]{:S(2)}) copy-start(bf16[8,2,2,512]{3,2,1,0:T(2,128)(2,1)} %param.8) | copy-start | bytes 98308
  0.7 3.7 %copy-start.7 = (s32[4]{0:T(128)S(1)}, s32[4]{0:T(128)}, u32[]{:S(2)}) copy-start(s32[4]{0:T(128)} %param.13) | copy-start | bytes 52
  0.7 3.7 %copy-start.6 = (f32[4]{0:T(128)S(1)}, f32[4]{0:T(128)}, u32[]{:S(2)}) copy-start(f32[4]{0:T(128)} %param.14) | copy-start | bytes 52
  9.2 6.8 %copy-start.3 = (bf16[8,2,2,512]{3,2,1,0:T(2,128)(2,1)S(1)}, bf16[8,2,2,512]{3,2,1,0:T(2,128)(2,1)}, u32[]{:S(2)}) copy-start(bf16[8,2,2,512]{3,2,1,0:T(2,128)(2,1)} %param.9) | copy-start | bytes 98308
  9.2 38.7 %copy-start.5 = (s32[80,2]{0,1:T(2,128)S(1)}, s32[80,2]{0,1:T(2,128)}, u32[]{:S(2)}) copy-start(s32[80,2]{0,1:T(2,128)} %param.15) | copy-start | bytes 1924
  9.2 38.8 %copy-start.4 = (f32[2,3]{1,0:T(2,128)S(1)}, f32[2,3]{1,0:T(2,128)}, u32[]{:S(2)}) copy-start(f32[2,3]{1,0:T(2,128)} %param.11) | copy-start | bytes 76
  11.5 40.5 %collective-permute-start = (bf16[8,1,2,512]{3,0,2,1:T(8,128)(2,1)S(1)}, bf16[8,1,2,512]{3,0,2,1:T(8,128)(2,1)S(1)}, u32[]{:S(2)}, u32[]{:S(2)}) collective-permute-start(bf16[8,1,2,512]{3,0,2,1:T(8,128)(2,1)S(1)} %get-tuple-element.22), channel_id=1, source_target_pairs={{0,1},{1,2},{2,3},{4,5},{5,6},{6,7},{8,9},{9,10},{10,11},{12,13},{... | collective-permute-start | bytes 49160 | tf_op jit(solution)/shard_map/ppermute | solution.py:17
  13.9 38.1 %collective-permute-start.1 = (bf16[8,1,2,512]{3,0,2,1:T(8,128)(2,1)S(1)}, bf16[8,1,2,512]{3,0,2,1:T(8,128)(2,1)S(1)}, u32[]{:S(2)}, u32[]{:S(2)}) collective-permute-start(bf16[8,1,2,512]{3,0,2,1:T(8,128)(2,1)S(1)} %get-tuple-element.23), channel_id=1, source_target_pairs={{1,0},{2,1},{3,2},{5,4},{6,5},{7,6},{9,8},{10,9},{11,10},{13,12},{... | collective-permute-start | bytes 49160 | tf_op jit(solution)/shard_map/ppermute | solution.py:18
  68.5 4.2 %collective-permute-start.2 = (bf16[8,1,2,512]{3,0,2,1:T(8,128)(2,1)S(1)}, bf16[8,1,2,512]{3,0,2,1:T(8,128)(2,1)S(1)}, u32[]{:S(2)}, u32[]{:S(2)}) collective-permute-start(bf16[8,1,2,512]{3,0,2,1:T(8,128)(2,1)S(1)} %get-tuple-element.20), channel_id=1, source_target_pairs={{0,1},{1,2},{2,3},{4,5},{5,6},{6,7},{8,9},{9,10},{10,11},{12,13},{... | collective-permute-start | bytes 49160 | tf_op jit(solution)/shard_map/ppermute | solution.py:17
  70.8 4.6 %collective-permute-start.3 = (bf16[8,1,2,512]{3,0,2,1:T(8,128)(2,1)S(1)}, bf16[8,1,2,512]{3,0,2,1:T(8,128)(2,1)S(1)}, u32[]{:S(2)}, u32[]{:S(2)}) collective-permute-start(bf16[8,1,2,512]{3,0,2,1:T(8,128)(2,1)S(1)} %get-tuple-element.21), channel_id=1, source_target_pairs={{1,0},{2,1},{3,2},{5,4},{6,5},{7,6},{9,8},{10,9},{11,10},{13,12},{... | collective-permute-start | bytes 49160 | tf_op jit(solution)/shard_map/ppermute | solution.py:18
where the time goes:
time: 118 us
  blocking collectives  76.7 us (65%)
  other arithmetic  17.5 us (15%)
  local copies, waits for them, and re-layouts  8.32 us (7%)
  starting transfers between devices  7.2 us (6%)
  matrix products  4.26 us (4%)
  waiting for transfers between devices  2.63 us (2%)
    psum x1, blocking collectives, body(): summed = lax.psum(partial_grad, 'mode')  37.1 us
    all_gather x1, blocking collectives, body(): shard_rows = lax.all_gather(backward, 'mode', axis=0, tiled=True)  31.9 us
    psum x1, blocking collectives, body(): match_sum = lax.psum(block, 'row')  7.74 us
    ppermute x2, starting transfers between devices, padded_2(): before = lax.ppermute(last, axis, up)  4.61 us
    another operation x2, other arithmetic  3.81 us
    neg x1, other arithmetic, times_minus_i(): return jnp.stack([fields[:, :, 1], -fields[:, :, 0]], axis=2)  3.74 us
    slice x1, other arithmetic, times_minus_i(): return jnp.stack([fields[:, :, 1], -fields[:, :, 0]], axis=2)  3.74 us
    dot_general x2, matrix products, propagate(): jnp.dot(fields.reshape(-1, 2 * width), matrix, preferred_element_type=jnp...  2.92 us
  transfers between devices with their start and end apart: 4, of which 1 were waited for; matrix products, arithmetic and copies ran while one was open for 5% of the time, Pallas kernels for 0%

commit v1 on v0

--- a/solution.py
+++ b/solution.py
@@ -5,6 +5,24 @@
 from jax.sharding import PartitionSpec as P
 
 NG = 16
+
+
+def in_order(blocks, dim):
+    blocks = jnp.moveaxis(blocks, 0, dim)
+    shape = blocks.shape
+    return blocks.reshape(*shape[:dim], shape[dim] * shape[dim + 1], *shape[dim + 2 :])
+
+
+def doubled(array, axis):
+    size = lax.axis_size(axis)
+    blocks = array[None]
+    for level in range(size.bit_length() - 1):
+        stride = 1 << level
+        received = lax.ppermute(blocks, axis, [(i, i ^ stride) for i in range(size)])
+        both = jnp.stack([blocks, received])
+        upper = lax.axis_index(axis) >> level & 1
+        blocks = jnp.where(upper == 0, both, both[::-1]).reshape(-1, *array.shape)
+    return blocks
 
 
 def padded_2(array, sides, width):
@@ -115,7 +133,7 @@
     target_onehot = (target_groups[:, None] == group_ids[None, :]).astype(jnp.float32)
     own_pairs = jnp.dot(own_onehot, pair_matrix.T, precision=lax.Precision.HIGHEST)
     column_mask = jnp.dot(own_pairs, target_onehot.T, precision=lax.Precision.HIGHEST)
-    shard_rows = lax.all_gather(backward, "mode", axis=0, tiled=True)
+    shard_rows = in_order(doubled(backward, "mode"), 0)
     rows_flat = shard_rows.reshape(shard_rows.shape[0], -1)
     real_part = jnp.einsum("nd,kd->nk", field_flat, rows_flat, preferred_element_type=jnp.float32)
     imag_part = jnp.einsum("nd,kd->nk", field_turned, rows_flat, preferred_element_type=jnp.float32)

time: 118 us -> 128 us (1.085)
  waiting for transfers between devices: 2.63 us -> 7.51 us
  other arithmetic: 17.5 us -> 21.6 us
  blocking collectives: 76.7 us -> 73.9 us
  starting transfers between devices: 7.2 us -> 9.71 us
    ppermute x0 -> x3, waiting for transfers between devices: none -> 4.88 us  [doubled(): lax.ppermute(blocks, axis, [(i, i ^ stride) for i in range(size)])]
    ppermute x0 -> x3, starting transfers between devices: none -> 2.53 us  [doubled(): lax.ppermute(blocks, axis, [(i, i ^ stride) for i in range(size)])]
    another operation x2 -> x6, other arithmetic: 3.81 us -> 5.32 us
  transfers between devices with their start and end apart: 4 -> 7, of which waited for: 1 -> 3; matrix products, arithmetic and copies ran while one was open for 5% -> 12% of each run, Pallas kernels for 0% -> 0%
where the time goes in v1:
time: 128 us; the launch traced here: 127 us
  blocking collectives  73.9 us (58%)
  other arithmetic  21.6 us (17%)
  starting transfers between devices  9.71 us (8%)
  local copies, waits for them, and re-layouts  8.58 us (7%)
  waiting for transfers between devices  7.51 us (6%)
  matrix products  4.91 us (4%)
    psum x1, blocking collectives, body(): summed = lax.psum(partial_grad, 'mode')  36.1 us
    all_gather x1, blocking collectives, body(): shard_rows = lax.all_gather(backward, 'mode', axis=0, tiled=True)  31.2 us
    psum x1, blocking collectives, body(): match_sum = lax.psum(block, 'row')  6.63 us
    ppermute x3, waiting for transfers between devices, doubled(): lax.ppermute(blocks, axis, [(i, i ^ stride) for i in range(size)])  4.88 us
    ppermute x2, starting transfers between devices, padded_2(): before = lax.ppermute(last, axis, up)  4.6 us
    another operation x2, other arithmetic  3.83 us
    neg x1, other arithmetic, times_minus_i(): return jnp.stack([fields[:, :, 1], -fields[:, :, 0]], axis=2)  3.82 us
    slice x1, other arithmetic, times_minus_i(): return jnp.stack([fields[:, :, 1], -fields[:, :, 0]], axis=2)  3.82 us
  transfers between devices with their start and end apart: 7, of which 3 were waited for; matrix products, arithmetic and copies ran while one was open for 12% of the time, Pallas kernels for 0%

profile of v1, /device:TPU:0, one launch (start us, length us, event | category | flops | bytes accessed | tf_op | source)
XLA Modules:
  0.0 127.3 jit_solution(5459791669109771450)
XLA Ops:
  0.6 0.0 copy-start
  0.6 0.0 copy-start.1
  0.7 0.0 copy-start.3
  0.7 0.0 copy-start.10
  0.7 0.0 copy-start.9
  0.7 2.7 %slice_bitcast_fusion = (bf16[512,512]{0,1:T(8,128)(2,1)}, bf16[512,512]{0,1:T(8,128)(2,1)}, bf16[512,512]{1,0:T(8,128)(2,1)}, bf16[512,512]{1,0:T(8,128)(2,1)}) fusion(bf16[2,512,512]{2,1,0:T(8,128)(2,1)} %param.10), kind=kLoop, calls=%fused_computation.11 | loop fusion | bytes 3145728 | tf_op jit(solution)/shard_map/transpose | solution.py:68
  3.4 0.0 copy-done.1
  3.4 0.8 fusion.13
  4.3 0.3 fusion.20
  4.7 1.8 %maximum_bitcast_fusion = bf16[1024,1024]{0,1:T(8,128)(2,1)S(1)} fusion(bf16[512,512]{1,0:T(8,128)(2,1)} %get-tuple-element.13, bf16[512,512]{1,0:T(8,128)(2,1)} %fusion.13, bf16[512,512]{1,0:T(8,128)(2,1)} %get-tuple-element.12), kind=kLoop, calls=%fused_computation.3 | loop fusion | flops 8388608 | bytes 3670016 | tf_op jit(solution)/shard_map/dot_general | solution.py:75
  6.5 2.6 %copy.22 = bf16[1024,1024]{1,0:T(8,128)(2,1)} copy(bf16[1024,1024]{0,1:T(8,128)(2,1)S(1)} %maximum_bitcast_fusion) | data formatting | bytes 4194304 | tf_op jit(solution)/shard_map/dot_general | solution.py:75
  9.1 2.3 %convolution_convert_fusion = bf16[8,2,2,512]{3,0,2,1:T(8,128)(2,1)S(1)} fusion(bf16[8,2,1024,1]{2,0,3,1:T(8,128)(2,1)S(1)} %bitcast.104, bf16[2,512,1024,1]{2,1,0,3:T(8,128)(2,1)} %bitcast.99), kind=kOutput, calls=%fused_computation.5 | convolution fusion | flops 33570816 | bytes 2162688 | tf_op jit(solution)/shard_map/dot_general | solution.py:75
  11.4 0.6 fusion.18
  12.0 2.3 %collective-permute-start = (bf16[8,1,2,512]{3,0,2,1:T(8,128)(2,1)}, bf16[8,1,2,512]{3,0,2,1:T(8,128)(2,1)S(1)}, u32[]{:S(2)}, u32[]{:S(2)}) collective-permute-start(bf16[8,1,2,512]{3,0,2,1:T(8,128)(2,1)} %get-tuple-element.24), channel_id=1, source_target_pairs={{0,1},{1,2},{2,3},{4,5},{5,6},{6,7},{8,9},{9,10},{10,11},{12,13},{... | collective-permute-start | bytes 49160 | tf_op jit(solution)/shard_map/ppermute | solution.py:35
  14.4 1.3 %collective-permute-start.1 = (bf16[8,1,2,512]{3,0,2,1:T(8,128)(2,1)}, bf16[8,1,2,512]{3,0,2,1:T(8,128)(2,1)}, u32[]{:S(2)}, u32[]{:S(2)}) collective-permute-start(bf16[8,1,2,512]{3,0,2,1:T(8,128)(2,1)} %get-tuple-element.25), channel_id=1, source_target_pairs={{1,0},{2,1},{3,2},{5,4},{6,5},{7,6},{9,8},{10,9},{11,10},{13,12},{... | collective-permute-start | bytes 49160 | tf_op jit(solution)/shard_map/ppermute | solution.py:36
  15.7 2.4 %collective-permute-start.2 = (bf16[1,8,2,2,512]{4,3,2,1,0:T(2,128)(2,1)S(1)}, bf16[1,8,2,2,512]{4,3,2,1,0:T(2,128)(2,1)}, u32[]{:S(2)}, u32[]{:S(2)}) collective-permute-start(bf16[1,8,2,2,512]{4,3,2,1,0:T(2,128)(2,1)S(1)} %bitcast.109), channel_id=1, source_target_pairs={{0,4},{4,0},{8,12},{12,8},{16,20},{20,16},{24,28},{28,24},{1,5},{5... | collective-permute-start | bytes 98312 | tf_op jit(solution)/shard_map/ppermute | solution.py:21
  18.1 31.2 %all_gather.3 = bf16[64,2,2,512]{3,2,1,0:T(2,128)(2,1)S(1)} all-gather(bf16[8,2,2,512]{3,2,1,0:T(2,128)(2,1)S(1)} %copy-done.4), channel_id=1, replica_groups=mesh['mode'=8,'row'=4] {'mode'}, dimensions={0}, use_global_device_ids=true | all-gather | bytes 294912 | tf_op jit(solution)/shard_map/all_gather | solution.py:144
  49.2 0.8 fusion.14
  50.1 0.0 copy-done.8
  50.1 0.6 slice_negate_fusion
  50.7 0.0 copy-done.5
  50.7 0.5 slice_negate_fusion.1
  51.3 0.1 convert_reduce_fusion
  51.4 0.2 fusion.5
  51.6 0.8 convolution_multiply_fusion.1
  52.4 0.6 pad_maximum_fusion.1
  53.0 1.6 %maximum_maximum_fusion = bf16[1024,1024]{0,1:T(8,128)(2,1)S(1)} fusion(bf16[512,512]{0,1:T(8,128)(2,1)} %get-tuple-element.11, bf16[512,512]{0,1:T(8,128)(2,1)} %get-tuple-element.10, bf16[512,512]{0,1:T(8,128)(2,1)S(1)} %copy-done.2), kind=kLoop, calls=%fused_computation.4 | loop fusion | flops 8388608 | bytes 3670016 | tf_op jit(solution)/shard_map/concatenate | solution.py:70
  54.6 0.7 fusion.21
  55.3 0.2 reshape.187
  55.5 0.0 copy-start.7
  55.5 0.2 reshape.188
  55.7 0.0 collective-permute-done
  55.7 0.0 collective-permute-done.1
  55.7 0.7 maximum_convert_fusion
  56.5 0.0 collective-permute-done.2
  56.5 0.9 pad_maximum_fusion.3
  57.3 0.1 fusion.7
  57.4 0.0 copy-start.6
  57.4 0.1 collective-permute-start.3
  57.5 3.8 %fusion.16 = (bf16[8,2,1,512]{3,0,2,1:T(8,128)(2,1)S(1)}, bf16[8,2,1,512]{3,0,2,1:T(8,128)(2,1)S(1)}) fusion(f32[8,4,2,512]{3,0,2,1:T(8,128)S(1)} %maximum_convert_fusion, f32[]{:T(128)} %bitcast.16, f32[]{:T(128)} %bitcast.15, f32[]{:T(128)} %bitcast.14, f32[]{:T(128)} %bitcast.13, f32[]{:T(128)} %bitcast.12, f32[]{:T(128)} %bitcast), kind=kLoop, calls=%fused_computation.72 | loop fusion | flops 106496 | bytes 229400 | tf_op jit(solution)/shard_map/neg | solution.py:109
  61.3 1.6 %collective-permute-done.3 = bf16[2,8,2,2,512]{4,3,2,1,0:T(2,128)(2,1)S(1)} collective-permute-done((bf16[2,8,2,2,512]{4,3,2,1,0:T(2,128)(2,1)S(1)}, bf16[2,8,2,2,512]{4,3,2,1,0:T(2,128)(2,1)S(1)}, u32[]{:S(2)}, u32[]{:S(2)}) %collective-permute-start.3) | collective-permute-done | bytes 65568 | tf_op jit(solution)/shard_map/ppermute | solution.py:21
  63.0 0.2 pad_maximum_fusion.2
  63.2 0.1 broadcast_select_fusion.1
  63.3 0.1 collective-permute-start.4
  63.4 3.8 %add_convert_fusion.1 = bf16[8,2,1,512]{3,0,2,1:T(8,128)(2,1)S(1)} fusion(f32[8,4,2,512]{3,0,2,1:T(8,128)S(1)} %maximum_convert_fusion, f32[]{:T(128)} %bitcast.16, f32[]{:T(128)} %bitcast.15, f32[]{:T(128)} %bitcast.14, f32[]{:T(128)} %bitcast.13, f32[]{:T(128)} %bitcast.12, f32[]{:T(128)} %bitcast), kind=kLoop, calls=%fused_computation.35 | loop fusion | flops 98304 | bytes 213016 | tf_op jit(solution)/shard_map/slice | solution.py:109
  67.2 3.2 %collective-permute-done.4 = bf16[4,8,2,2,512]{4,3,2,1,0:T(2,128)(2,1)S(1)} collective-permute-done((bf16[4,8,2,2,512]{4,3,2,1,0:T(2,128)(2,1)S(1)}, bf16[4,8,2,2,512]{4,3,2,1,0:T(2,128)(2,1)S(1)}, u32[]{:S(2)}, u32[]{:S(2)}) %collective-permute-start.4) | collective-permute-done | bytes 131104 | tf_op jit(solution)/shard_map/ppermute | solution.py:21
  70.4 0.4 pad_maximum_fusion
  70.8 0.2 broadcast_select_fusion
  71.1 0.2 reshape_reshape_reshape.3
  71.2 0.2 convolution_bitcast_fusion.1
  71.4 0.2 convolution_bitcast_fusion
  71.6 6.6 %psum.14 = f32[2,8,64]{2,1,0:T(8,128)S(1)} all-reduce(f32[2,8,64]{2,1,0:T(8,128)S(1)} %pad_maximum_fusion.7), channel_id=1, replica_groups=mesh['mode'=8,'row'=4] {'row'}, use_global_device_ids=true, to_apply=%region_0.0 | all-reduce | flops 1024 | bytes 8192 | tf_op jit(solution)/shard_map/psum | solution.py:141
  78.3 0.6 fusion.15
  78.9 0.1 fusion.8
  79.0 0.2 fusion.1
  79.2 2.3 %collective-permute-start.5 = (bf16[8,1,2,512]{3,0,2,1:T(8,128)(2,1)S(1)}, bf16[8,1,2,512]{3,0,2,1:T(8,128)(2,1)S(1)}, u32[]{:S(2)}, u32[]{:S(2)}) collective-permute-start(bf16[8,1,2,512]{3,0,2,1:T(8,128)(2,1)S(1)} %get-tuple-element.22), channel_id=1, source_target_pairs={{0,1},{1,2},{2,3},{4,5},{5,6},{6,7},{8,9},{9,10},{10,11},{12,13},{... | collective-permute-start | bytes 49160 | tf_op jit(solution)/shard_map/ppermute | solution.py:35
  81.4 1.3 %collective-permute-start.6 = (bf16[8,1,2,512]{3,0,2,1:T(8,128)(2,1)S(1)}, bf16[8,1,2,512]{3,0,2,1:T(8,128)(2,1)S(1)}, u32[]{:S(2)}, u32[]{:S(2)}) collective-permute-start(bf16[8,1,2,512]{3,0,2,1:T(8,128)(2,1)S(1)} %get-tuple-element.23), channel_id=1, source_target_pairs={{1,0},{2,1},{3,2},{5,4},{6,5},{7,6},{9,8},{10,9},{11,10},{13,12},{... | collective-permute-start | bytes 49160 | tf_op jit(solution)/shard_map/ppermute | solution.py:36
  82.7 0.7 fusion.22
  83.4 0.0 collective-permute-done.5
  83.4 2.6 %collective-permute-done.6 = bf16[8,1,2,512]{3,0,2,1:T(8,128)(2,1)S(1)} collective-permute-done((bf16[8,1,2,512]{3,0,2,1:T(8,128)(2,1)S(1)}, bf16[8,1,2,512]{3,0,2,1:T(8,128)(2,1)S(1)}, u32[]{:S(2)}, u32[]{:S(2)}) %collective-permute-start.6) | collective-permute-done | bytes 16416 | tf_op jit(solution)/shard_map/ppermute | solution.py:36
  86.1 3.8 %subtract_convert_fusion = (bf16[8,2,1,512]{3,0,2,1:T(8,128)(2,1)S(1)}, bf16[8,2,1,512]{3,0,2,1:T(8,128)(2,1)S(1)}) fusion(f32[8,4,2,512]{3,0,2,1:T(8,128)S(1)} %maximum_convert_fusion.1, f32[]{:T(128)} %bitcast.37, f32[]{:T(128)} %bitcast.36, f32[]{:T(128)} %bitcast.35, f32[]{:T(128)} %bitcast.15, f32[]{:T(128)} %bitcast.13, f32[]{:T(128)} %bitcast), kind=kLoop, calls=%fused_computation.33 | loop fusion | flops 196608 | bytes 229400 | tf_op jit(solution)/shard_map/convert.1
  89.9 0.6 fusion.23
  90.6 36.1 %psum.15 = f32[4,2,512]{2,0,1:T(4,128)S(1)} all-reduce(f32[4,2,512]{2,0,1:T(4,128)S(1)} %reduce_sum.19), channel_id=1, replica_groups=mesh['mode'=8,'row'=4] {'mode'}, use_global_device_ids=true, to_apply=%region_3.4 | all-reduce | flops 4096 | bytes 32768 | tf_op jit(solution)/shard_map/psum | solution.py:163
  126.7 0.6 copy.23
  (32 shorter events, 0.3 us)
Async XLA Ops:
  0.6 3.7 %copy-start = (f32[7,2,512]{2,1,0:T(2,128)S(1)}, f32[7,2,512]{2,1,0:T(2,128)}, u32[]{:S(2)}) copy-start(f32[7,2,512]{2,1,0:T(2,128)} %param.12) | copy-start | bytes 86020
  0.6 2.8 %copy-start.1 = (bf16[2,512,512]{2,1,0:T(8,128)(2,1)S(1)}, bf16[2,512,512]{2,1,0:T(8,128)(2,1)}, u32[]{:S(2)}) copy-start(bf16[2,512,512]{2,1,0:T(8,128)(2,1)} %param.10) | copy-start | bytes 3145732
  0.7 3.6 %copy-start.3 = (bf16[8,2,2,512]{3,2,1,0:T(2,128)(2,1)S(1)}, bf16[8,2,2,512]{3,2,1,0:T(2,128)(2,1)}, u32[]{:S(2)}) copy-start(bf16[8,2,2,512]{3,2,1,0:T(2,128)(2,1)} %param.8) | copy-start | bytes 98308
  0.7 3.6 %copy-start.10 = (s32[4]{0:T(128)S(1)}, s32[4]{0:T(128)}, u32[]{:S(2)}) copy-start(s32[4]{0:T(128)} %param.13) | copy-start | bytes 52
  0.7 3.6 %copy-start.9 = (f32[4]{0:T(128)S(1)}, f32[4]{0:T(128)}, u32[]{:S(2)}) copy-start(f32[4]{0:T(128)} %param.14) | copy-start | bytes 52
  9.1 6.6 %copy-start.4 = (bf16[8,2,2,512]{3,2,1,0:T(2,128)(2,1)S(1)}, bf16[8,2,2,512]{3,2,1,0:T(2,128)(2,1)}, u32[]{:S(2)}) copy-start(bf16[8,2,2,512]{3,2,1,0:T(2,128)(2,1)} %param.9) | copy-start | bytes 98308
  9.1 41.0 %copy-start.8 = (s32[80,2]{0,1:T(2,128)S(1)}, s32[80,2]{0,1:T(2,128)}, u32[]{:S(2)}) copy-start(s32[80,2]{0,1:T(2,128)} %param.15) | copy-start | bytes 1924
  9.1 41.6 %copy-start.5 = (f32[2,3]{1,0:T(2,128)S(1)}, f32[2,3]{1,0:T(2,128)}, u32[]{:S(2)}) copy-start(f32[2,3]{1,0:T(2,128)} %param.11) | copy-start | bytes 76
  12.0 43.7 %collective-permute-start = (bf16[8,1,2,512]{3,0,2,1:T(8,128)(2,1)}, bf16[8,1,2,512]{3,0,2,1:T(8,128)(2,1)S(1)}, u32[]{:S(2)}, u32[]{:S(2)}) collective-permute-start(bf16[8,1,2,512]{3,0,2,1:T(8,128)(2,1)} %get-tuple-element.24), channel_id=1, source_target_pairs={{0,1},{1,2},{2,3},{4,5},{5,6},{6,7},{8,9},{9,10},{10,11},{12,13},{... | collective-permute-start | bytes 49160 | tf_op jit(solution)/shard_map/ppermute | solution.py:35
  14.4 41.3 %collective-permute-start.1 = (bf16[8,1,2,512]{3,0,2,1:T(8,128)(2,1)}, bf16[8,1,2,512]{3,0,2,1:T(8,128)(2,1)}, u32[]{:S(2)}, u32[]{:S(2)}) collective-permute-start(bf16[8,1,2,512]{3,0,2,1:T(8,128)(2,1)} %get-tuple-element.25), channel_id=1, source_target_pairs={{1,0},{2,1},{3,2},{5,4},{6,5},{7,6},{9,8},{10,9},{11,10},{13,12},{... | collective-permute-start | bytes 49160 | tf_op jit(solution)/shard_map/ppermute | solution.py:36
  15.7 40.8 %collective-permute-start.2 = (bf16[1,8,2,2,512]{4,3,2,1,0:T(2,128)(2,1)S(1)}, bf16[1,8,2,2,512]{4,3,2,1,0:T(2,128)(2,1)}, u32[]{:S(2)}, u32[]{:S(2)}) collective-permute-start(bf16[1,8,2,2,512]{4,3,2,1,0:T(2,128)(2,1)S(1)} %bitcast.109), channel_id=1, source_target_pairs={{0,4},{4,0},{8,12},{12,8},{16,20},{20,16},{24,28},{28,24},{1,5},{5... | collective-permute-start | bytes 98312 | tf_op jit(solution)/shard_map/ppermute | solution.py:21
  50.1 2.9 %copy-start.2 = (bf16[512,512]{0,1:T(8,128)(2,1)S(1)}, bf16[512,512]{0,1:T(8,128)(2,1)}, u32[]{:S(2)}) copy-start(bf16[512,512]{0,1:T(8,128)(2,1)} %fusion.14) | copy-start | bytes 1572868
  55.5 22.7 %copy-start.7 = (f32[8,64]{1,0:T(8,128)S(1)}, f32[8,64]{1,0:T(8,128)}, u32[]{:S(2)}) copy-start(f32[8,64]{1,0:T(8,128)} %convolution_multiply_fusion.1) | copy-start | bytes 6148
  57.4 25.3 %copy-start.6 = (f32[1,3]{1,0:T(1,128)S(1)}, f32[1,3]{1,0:T(1,128)}, u32[]{:S(2)}) copy-start(f32[1,3]{1,0:T(1,128)} %slice_negate_fusion.1) | copy-start | bytes 40
  57.4 5.6 %collective-permute-start.3 = (bf16[2,8,2,2,512]{4,3,2,1,0:T(2,128)(2,1)S(1)}, bf16[2,8,2,2,512]{4,3,2,1,0:T(2,128)(2,1)S(1)}, u32[]{:S(2)}, u32[]{:S(2)}) collective-permute-start(bf16[2,8,2,2,512]{4,3,2,1,0:T(2,128)(2,1)S(1)} %get-tuple-element.21), channel_id=1, source_target_pairs={{0,8},{4,12},{8,0},{12,4},{16,24},{20,28},{24,16},{28,20},{1,9},{5... | collective-permute-start | bytes 196616 | tf_op jit(solution)/shard_map/ppermute | solution.py:21
  63.3 7.2 %collective-permute-start.4 = (bf16[4,8,2,2,512]{4,3,2,1,0:T(2,128)(2,1)S(1)}, bf16[4,8,2,2,512]{4,3,2,1,0:T(2,128)(2,1)S(1)}, u32[]{:S(2)}, u32[]{:S(2)}) collective-permute-start(bf16[4,8,2,2,512]{4,3,2,1,0:T(2,128)(2,1)S(1)} %bitcast.100), channel_id=1, source_target_pairs={{0,16},{4,20},{8,24},{12,28},{16,0},{20,4},{24,8},{28,12},{1,17},{... | collective-permute-start | bytes 393224 | tf_op jit(solution)/shard_map/ppermute | solution.py:21
  79.2 4.2 %collective-permute-start.5 = (bf16[8,1,2,512]{3,0,2,1:T(8,128)(2,1)S(1)}, bf16[8,1,2,512]{3,0,2,1:T(8,128)(2,1)S(1)}, u32[]{:S(2)}, u32[]{:S(2)}) collective-permute-start(bf16[8,1,2,512]{3,0,2,1:T(8,128)(2,1)S(1)} %get-tuple-element.22), channel_id=1, source_target_pairs={{0,1},{1,2},{2,3},{4,5},{5,6},{6,7},{8,9},{9,10},{10,11},{12,13},{... | collective-permute-start | bytes 49160 | tf_op jit(solution)/shard_map/ppermute | solution.py:35
  81.4 4.6 %collective-permute-start.6 = (bf16[8,1,2,512]{3,0,2,1:T(8,128)(2,1)S(1)}, bf16[8,1,2,512]{3,0,2,1:T(8,128)(2,1)S(1)}, u32[]{:S(2)}, u32[]{:S(2)}) collective-permute-start(bf16[8,1,2,512]{3,0,2,1:T(8,128)(2,1)S(1)} %get-tuple-element.23), channel_id=1, source_target_pairs={{1,0},{2,1},{3,2},{5,4},{6,5},{7,6},{9,8},{10,9},{11,10},{13,12},{... | collective-permute-start | bytes 49160 | tf_op jit(solution)/shard_map/ppermute | solution.py:36
